TPU v7x, 512 devices: a whole 4x8x8 slice. The times are simulated.
512 devices in a mesh: dof: 64 (over z, y_lo, core), real: 8 (over y_hi, x).
Axes of the slice: x: 4, y: 8 (y_hi: 2, y_lo: 4; y = y_hi * 4 + y_lo), z: 8, core: 2. Of those that a mesh axis runs over, the one named last changes fastest.
Arguments:
- mode_panel: bfloat16 [131072, 512], P('dof'), may hold values from -0.31445312 to 0.31445312
- stiff_blocks: bfloat16 [1024, 5, 128, 128], P('dof'), as said below
- stiff_cols: int32 [1024, 5], P('dof'), may hold values from 0 to 1023, as said below
- row_blade: int32 [131072], P('dof'), may hold values from 0 to 3, as said below
- adjusted_values: float32 [512], replicated, may hold values from 4 to 24
- deviations: float32 [128, 4], P('dof'), may hold values from -0.05 to 0.05
- start_block: float32 [512, 128], P('real'), may hold values from -6 to 6
Outputs:
- projected: float32 [4, 512, 512], P(None, 'real')
- subspace: float32 [128, 512, 128], P('dof', 'real')
Inputs may be any that keep to these rules, and one draw needn't show every extreme that they name: `stiff_cols`: each block row's 5 entries are, in some order, the block row itself and the block rows two and one before and one and two after it; where one of those lies outside the grid or in another blade's rows, the block row itself stands in. `stiff_blocks`: the stiffness is symmetric and couples no two blades: the block of block row g at column c is the transpose of the block of block row c at column g, diagonal blocks are symmetric, and stand-in blocks are zero. `row_blade`: block row g belongs to the blade numbered ((g + 8) // 256) mod 4 under a fixed relabelling of the blades; so each blade owns a run of 32768 neighbouring rows, except one blade, which owns the first 31744 rows and the last 1024 rows.
All inputs are finite; a program needn't handle non-finite values.
Results may differ from a plain program's by a relative error of at most 0.003.
Values may be sent and summed in bfloat16 or wider, within the bound.
No kernel may reach another device: no remote copies, remote signals or barrier semaphores. Data moves between devices by JAX's collectives and lax.ppermute only.
A program may use at most 64 MiB of HBM per device.

v0:
```python
import jax
import jax.numpy as jnp
from jax import lax
from jax.sharding import PartitionSpec as P

ADJUSTED_MODES = 512
NBLADE = 4
STEPS = 2
highest_accuracy = lax.Precision.HIGHEST


def with_halo(block, sides, width):
    for axis, dim in sides:
        count = lax.axis_size(axis)
        forward = [(i, i + 1) for i in range(count - 1)]
        backward = [(target, source) for source, target in forward]
        low = lax.ppermute(
            lax.slice_in_dim(block, block.shape[dim] - width, None, axis=dim), axis, forward
        )
        high = lax.ppermute(lax.slice_in_dim(block, 0, width, axis=dim), axis, backward)
        block = jnp.concatenate([low, block, high], axis=dim)
    return block


def multiply_by_blocks(ext_blocks, blocks, columns):
    number = blocks.shape[0]
    size = blocks.shape[2]
    mode_count = ext_blocks.shape[2]
    row_totals = jnp.zeros((number, size, mode_count), jnp.float32)
    for slot_index in range(blocks.shape[1]):
        picked = jnp.take(ext_blocks, columns[:, slot_index], axis=0)
        row_totals = row_totals + jnp.einsum(
            "gab,gbm->gam", blocks[:, slot_index], picked, preferred_element_type=jnp.float32
        )
    return row_totals.reshape(number * size, mode_count).astype(jnp.bfloat16)


def add_projection(portion, offset, mode_panel, row_blade, col_start, owned_rows):
    number = portion.shape[0]
    left_rows = lax.dynamic_slice(mode_panel, (offset, col_start), (number, owned_rows))
    stacked = jnp.concatenate(
        [
            jnp.where((row_blade == blade_index)[:, None], left_rows, jnp.zeros_like(left_rows))
            for blade_index in range(NBLADE)
        ],
        axis=1,
    )
    return lax.dot_general(
        stacked, portion, (((0,), (0,)), ((), ())), preferred_element_type=jnp.float32
    )


def inverse_factor(inner_product_matrix):
    factor = jnp.linalg.cholesky(inner_product_matrix)
    identity = jnp.broadcast_to(
        jnp.eye(inner_product_matrix.shape[-1], dtype=inner_product_matrix.dtype),
        inner_product_matrix.shape,
    )
    return lax.linalg.triangular_solve(factor, identity, left_side=True, lower=True)


def normalize_parts(present_image):
    partial_inner_products = jnp.einsum(
        "eox,eol->exl", present_image, present_image, precision=highest_accuracy
    )
    inner_product_matrix = lax.psum(partial_inner_products, "real") / ADJUSTED_MODES
    inverse = inverse_factor(inner_product_matrix)
    return jnp.einsum("zjs,zts->zjt", present_image, inverse, precision=highest_accuracy)


def on_device(
    mode_panel, stiff_blocks, stiff_cols, row_blade, adjusted_values, deviations, start_block
):
    real_count = lax.axis_size("real")
    owner_index = lax.axis_index("real")
    mode_count = mode_panel.shape[1]
    owned_rows = mode_count // real_count
    block_size = stiff_blocks.shape[2]
    shard_blocks = stiff_blocks.shape[0]
    col_start = owner_index * owned_rows
    extended = with_halo(mode_panel, (("dof", 0),), 2 * block_size)
    ext_blocks = extended.reshape(shard_blocks + 4, block_size, mode_count)
    local_cols = stiff_cols - lax.axis_index("dof") * shard_blocks + 2
    stiff_image = multiply_by_blocks(ext_blocks, stiff_blocks, local_cols)
    blade_parts = add_projection(
        stiff_image, jnp.zeros((), jnp.int32), mode_panel, row_blade, col_start, owned_rows
    )
    summed = lax.psum(blade_parts, "dof")
    projected = summed.reshape(NBLADE, owned_rows, mode_count)
    row_ids = jnp.arange(owned_rows, dtype=jnp.int32) + col_start
    own_values = lax.dynamic_slice_in_dim(adjusted_values, col_start, owned_rows, 0)
    diagonal_part = jnp.where(
        jnp.arange(mode_count, dtype=jnp.int32)[None, :] == row_ids[:, None],
        own_values[:, None],
        jnp.zeros((), jnp.float32),
    )
    realizations = deviations.shape[0]
    subspace_width = start_block.shape[1]
    reduced = (
        jnp.einsum("zb,bjm->zjm", deviations, projected, precision=highest_accuracy)
        + diagonal_part[None]
    )
    current = jnp.broadcast_to(start_block[None], (realizations, owned_rows, subspace_width))
    for iteration in range(STEPS):
        present_image = jnp.einsum(
            "zjk,zks->zjs",
            reduced,
            lax.all_gather(current, "real", axis=1, tiled=True),
            precision=highest_accuracy,
        )
        current = normalize_parts(present_image)
    return (projected, current)


def solution(mesh):
    in_specs = (
        P("dof", None),
        P("dof", None, None, None),
        P("dof", None),
        P("dof"),
        P(),
        P("dof", None),
        P("real", None),
    )
    out_specs = (P(None, "real", None), P("dof", "real", None))
    return jax.shard_map(
        on_device, mesh=mesh, in_specs=in_specs, out_specs=out_specs, check_vma=False
    )
```

profile of v0, /device:TPU:64, one launch (start us, length us, event | category | flops | bytes accessed | tf_op | source)
XLA Modules:
  0.0 967.4 jit_solution(17578840527042316968)
XLA Ops:
  7.2 1.1 fusion.60
  8.3 1.9 collective-permute-start
  10.2 6.3 collective-permute-start.1
  18.0 5.4 broadcast_select_fusion.3
  24.4 2.0 gather_fusion.2
  26.4 2.0 gather_fusion.1
  28.4 2.0 gather_fusion.3
  30.4 2.0 gather_fusion.4
  32.4 2.0 gather_fusion
  34.5 2.7 fusion.3
  40.0 0.8 copy-done.4
  42.4 1.6 add_convert_fusion
  44.0 1.3 fusion.15
  45.3 1.1 copy.27
  46.6 44.8 %all_gather.8 = f32[512,128]{1,0:T(8,128)S(1)} all-gather(f32[64,128]{1,0:T(8,128)S(1)} %copy-done.12), channel_id=2, replica_groups=mesh['dof'=64,'real'=8] {'real'}, dimensions={0}, use_global_device_ids=true | all-gather | bytes 294912 | tf_op jit(solution)/shard_map/all_gather | solution.py:108
  91.5 492.6 %all-reduce.4.cloned.1.call-done = f32[4,64,512]{2,0,1:T(4,128)} async-done(((f32[4,64,512]{2,0,1:T(4,128)}), f32[4,64,512]{2,0,1:T(4,128)}) %all-reduce.4.cloned.1.call-update) | async-done | bytes 524304 | tf_op jit(solution)/shard_map/psum | solution.py:88
  584.2 2.1 fusion.14
  586.7 1.0 fusion.61
  588.0 125.4 %all-reduce.6.cloned.1.call-done = f32[2,128,128]{1,2,0:T(8,128)} async-done(((f32[2,128,128]{1,2,0:T(8,128)}), f32[2,128,128]{1,2,0:T(8,128)}) %all-reduce.6.cloned.1.call-update) | async-done | bytes 131088 | tf_op jit(solution)/shard_map/psum | solution.py:66
  713.4 0.9 broadcast_multiply_fusion.1
  714.4 0.9 fusion.48
  715.4 23.5 %custom-call.8 = f32[2,128,128]{2,1,0:T(8,128)S(1)} custom-call(f32[2,128,128]{2,1,0:T(8,128)S(1)} %fusion.48), custom_call_target="Cholesky" | custom-call | tf_op jit(solution)/shard_map/jit(cholesky)/cholesky | solution.py:54
  739.1 19.7 %custom-call.9 = f32[2,1,128,128]{2,3,1,0:T(8,128)S(1)} custom-call(f32[2,1,128,128]{3,2,1,0:T(8,128)S(1)} %select_bitcast_fusion.1), custom_call_target="InvertDiagBlocksLowerTriangular" | custom-call | tf_op jit(solution)/shard_map/triangular_solve/custom-call.0 | solution.py:59
  759.5 45.8 %all_gather.7 = f32[2,512,128]{2,1,0:T(8,128)S(1)} all-gather(f32[2,64,128]{2,1,0:T(8,128)S(1)} %fusion.62), channel_id=1, replica_groups=mesh['dof'=64,'real'=8] {'real'}, dimensions={1}, use_global_device_ids=true | all-gather | bytes 589824 | tf_op jit(solution)/shard_map/all_gather | solution.py:108
  805.8 1.0 fusion.63
  806.9 1.0 copy.34
  807.8 106.3 %all-reduce.8.cloned.1.call-done = f32[2,128,128]{1,2,0:T(8,128)} async-done(((f32[2,128,128]{1,2,0:T(8,128)}), f32[2,128,128]{1,2,0:T(8,128)}) %all-reduce.8.cloned.1.call-update) | async-done | bytes 131088 | tf_op jit(solution)/shard_map/psum | solution.py:66
  914.1 0.9 broadcast_multiply_fusion
  915.1 0.9 fusion.45
  916.0 23.5 %custom-call.10 = f32[2,128,128]{2,1,0:T(8,128)S(1)} custom-call(f32[2,128,128]{2,1,0:T(8,128)S(1)} %fusion.45), custom_call_target="Cholesky" | custom-call | tf_op jit(solution)/shard_map/jit(cholesky)/cholesky | solution.py:54
  939.8 19.7 %custom-call.11 = f32[2,1,128,128]{2,3,1,0:T(8,128)S(1)} custom-call(f32[2,1,128,128]{3,2,1,0:T(8,128)S(1)} %select_bitcast_fusion), custom_call_target="InvertDiagBlocksLowerTriangular" | custom-call | tf_op jit(solution)/shard_map/triangular_solve/custom-call.0 | solution.py:59
  959.8 1.0 fusion.64
  (62 shorter events, 10.0 us)
Async XLA Ops:
  7.2 577.0 %copy-start = (f32[2,4]{1,0:T(2,128)S(1)}, f32[2,4]{1,0:T(2,128)}, u32[]{:S(2)}) copy-start(f32[2,4]{1,0:T(2,128)} %param.17) | copy-start | bytes 100
  7.2 577.0 %all-reduce.4.cloned.1.call-start = ((), (), s32[]{:S(2)}) async-start(), calls=%async_computation | async-start | bytes 1048576 | tf_op jit(solution)/shard_map/psum | solution.py:88
  8.3 15.9 %collective-permute-start = (bf16[256,512]{1,0:T(8,128)(2,1)S(1)}, bf16[256,512]{1,0:T(8,128)(2,1)S(1)}, u32[]{:S(2)}, u32[]{:S(2)}) collective-permute-start(bf16[256,512]{1,0:T(8,128)(2,1)S(1)} %get-tuple-element.23), channel_id=1, source_target_pairs={{0,8},{8,16},{16,24},{24,32},{32,40},{40,48},{48,56},{56,64},{64,7... | collective-permute-start | bytes 786440 | tf_op jit(solution)/shard_map/ppermute | solution.py:17
  10.2 14.0 %collective-permute-start.1 = (bf16[256,512]{1,0:T(8,128)(2,1)S(1)}, bf16[256,512]{1,0:T(8,128)(2,1)S(1)}, u32[]{:S(2)}, u32[]{:S(2)}) collective-permute-start(bf16[256,512]{1,0:T(8,128)(2,1)S(1)} %get-tuple-element.24), channel_id=1, source_target_pairs={{8,0},{16,8},{24,16},{32,24},{40,32},{48,40},{56,48},{64,56},{72,6... | collective-permute-start | bytes 786440 | tf_op jit(solution)/shard_map/ppermute | solution.py:20
  18.0 6.2 copy-start.5
  34.5 2.7 copy-start.3
  34.5 3.2 copy-start.6
  37.6 1.6 copy-start.2
  39.2 1.6 copy-start.4
  40.8 1.6 copy-start.1
  42.4 1.6 copy-start.8
  42.4 1.6 copy-start.9
  42.4 1.6 copy-start.10
  42.4 1.6 copy-start.11
  44.0 2.5 copy-start.12
  46.5 666.9 %all-reduce.6.cloned.1.call-start = ((), (), s32[]{:S(2)}) async-start(), calls=%async_computation.1 | async-start | bytes 262144 | tf_op jit(solution)/shard_map/psum | solution.py:66
  586.7 220.2 %copy-start.7 = (f32[4,64,512]{2,0,1:T(4,128)S(1)}, f32[4,64,512]{2,0,1:T(4,128)}, u32[]{:S(2)}) copy-start(f32[4,64,512]{2,0,1:T(4,128)} %all-reduce.4.cloned.1.call-done) | copy-start | bytes 1572868
  587.8 326.3 %all-reduce.8.cloned.1.call-start = ((), (), s32[]{:S(2)}) async-start(), calls=%async_computation.2 | async-start | bytes 262144 | tf_op jit(solution)/shard_map/psum | solution.py:66
Sparse Core Ops, SparseCore 0:
  46.6 537.4 all-reduce.3
  587.9 125.4 all-reduce.5
  807.0 107.0 all-reduce.7
where the time goes:
time: 968 us; the launch traced here: 967 us
  waiting for transfers between devices  724 us (75%)
  other arithmetic  97.6 us (10%)
  blocking collectives  90.7 us (9%)
  local copies, waits for them, and re-layouts  17.1 us (2%)
  matrix products  15 us (2%)
  between operations  14.1 us (1%)
    psum x1, waiting for transfers between devices, on_device(): summed = lax.psum(blade_parts, 'dof')  493 us
    psum x2, waiting for transfers between devices, normalize_parts(): lax.psum(partial_inner_products, 'real') / ADJUSTED_MODES  232 us
    all_gather x2, blocking collectives, on_device(): lax.all_gather(current, 'real', axis=1, tiled=True)  90.7 us
    another operation x7, other arithmetic, inverse_factor(): factor = jnp.linalg.cholesky(inner_product_matrix)  47.2 us
    another operation x5, other arithmetic, inverse_factor(): lax.linalg.triangular_solve(factor, identity, left_side=True, lower=True)  39.6 us
  transfers between devices with their start and end apart: 5, of which 3 were waited for; matrix products, arithmetic and copies ran while one was open for 1% of the time, Pallas kernels for 0%

commit v1 on v0

--- a/solution.py
+++ b/solution.py
@@ -85,7 +85,7 @@
     blade_parts = add_projection(
         stiff_image, jnp.zeros((), jnp.int32), mode_panel, row_blade, col_start, owned_rows
     )
-    summed = lax.psum(blade_parts, "dof")
+    summed = jnp.sum(lax.all_gather(blade_parts, "dof"), axis=0)
     projected = summed.reshape(NBLADE, owned_rows, mode_count)
     row_ids = jnp.arange(owned_rows, dtype=jnp.int32) + col_start
     own_values = lax.dynamic_slice_in_dim(adjusted_values, col_start, owned_rows, 0)

time: 968 us -> 628 us (0.65)
  waiting for transfers between devices: 724 us -> 373 us
  other arithmetic: 97.6 us -> 111 us
    psum x1 -> x0, waiting for transfers between devices: 493 us -> none  [on_device(): summed = lax.psum(blade_parts, 'dof')]
    all_gather x0 -> x1, waiting for transfers between devices: none -> 152 us  [on_device(): summed = jnp.sum(lax.all_gather(blade_parts, 'dof'), axis=0)]
    reduce_sum x0 -> x1, other arithmetic: none -> 12.1 us  [on_device(): summed = jnp.sum(lax.all_gather(blade_parts, 'dof'), axis=0)]
    psum x2, waiting for transfers between devices: 232 us -> 221 us  [normalize_parts(): lax.psum(partial_inner_products, 'real') / ADJUSTED_MODES]
where the time goes in v1:
time: 628 us; the launch traced here: 627 us
  waiting for transfers between devices  373 us (59%)
  other arithmetic  111 us (18%)
  blocking collectives  91.1 us (15%)
  matrix products  15.1 us (2%)
  local copies, waits for them, and re-layouts  15 us (2%)
  between operations  14.1 us (2%)
  starting transfers between devices  8.56 us (1%)
    psum x2, waiting for transfers between devices, normalize_parts(): lax.psum(partial_inner_products, 'real') / ADJUSTED_MODES  221 us
    all_gather x1, waiting for transfers between devices, on_device(): summed = jnp.sum(lax.all_gather(blade_parts, 'dof'), axis=0)  152 us
    all_gather x2, blocking collectives, on_device(): lax.all_gather(current, 'real', axis=1, tiled=True)  91.1 us
    another operation x7, other arithmetic, inverse_factor(): factor = jnp.linalg.cholesky(inner_product_matrix)  47.2 us
    another operation x5, other arithmetic, inverse_factor(): lax.linalg.triangular_solve(factor, identity, left_side=True, lower=True)  39.6 us
  transfers between devices with their start and end apart: 5, of which 3 were waited for; matrix products, arithmetic and copies ran while one was open for 1% of the time, Pallas kernels for 0%

profile of v1, /device:TPU:64, one launch (start us, length us, event | category | flops | bytes accessed | tf_op | source)
XLA Modules:
  0.0 627.3 jit_solution(8035535605177183888)
XLA Ops:
  7.2 1.1 fusion.61
  8.3 1.9 collective-permute-start
  10.2 6.3 %collective-permute-start.1 = (bf16[256,512]{1,0:T(8,128)(2,1)S(1)}, bf16[256,512]{1,0:T(8,128)(2,1)}, u32[]{:S(2)}, u32[]{:S(2)}) collective-permute-start(bf16[256,512]{1,0:T(8,128)(2,1)S(1)} %get-tuple-element.20), channel_id=1, source_target_pairs={{8,0},{16,8},{24,16},{32,24},{40,32},{48,40},{56,48},{64,56},{72,6... | collective-permute-start | bytes 786440 | tf_op jit(solution)/shard_map/ppermute | solution.py:20
  18.0 5.3 broadcast_select_fusion.3
  23.4 1.1 pad_maximum_fusion
  24.5 2.0 gather_fusion.2
  26.5 2.0 gather_fusion.1
  28.6 2.0 gather_fusion.3
  30.5 2.0 gather_fusion.4
  32.6 2.0 gather_fusion
  34.6 2.7 fusion.3
  40.1 0.8 copy-done.4
  42.6 1.6 add_convert_fusion
  44.2 2.1 fusion.15
  47.1 45.2 %all_gather.16 = f32[512,128]{1,0:T(8,128)S(1)} all-gather(f32[64,128]{1,0:T(8,128)S(1)} %copy-done.11), channel_id=2, replica_groups=mesh['dof'=64,'real'=8] {'real'}, dimensions={0}, use_global_device_ids=true | all-gather | bytes 294912 | tf_op jit(solution)/shard_map/all_gather | solution.py:108
  92.4 151.8 %all-gather.3.cloned.1.call-done = f32[16384,512]{1,0:T(8,128)} async-done(((f32[256,512]{1,0:T(8,128)}), f32[16384,512]{1,0:T(8,128)}) %all-gather.3.cloned.1.call-update) | async-done | bytes 33554448 | tf_op jit(solution)/shard_map/all_gather | solution.py:88
  244.2 12.1 %reduce_sum.9 = f32[256,512]{1,0:T(8,128)S(1)} reduce(f32[64,256,512]{2,1,0:T(8,128)} %bitcast.84, f32[]{:T(128)} %constant.71.clone.1), dimensions={0}, to_apply=%region_0.0 | reduce | flops 8257536 | bytes 34078724 | tf_op jit(solution)/shard_map/reduce_sum | solution.py:88
  256.3 1.3 fusion.14
  258.1 1.1 fusion.62
  259.5 113.8 %all-reduce.3.cloned.1.call-done = f32[2,128,128]{1,2,0:T(8,128)} async-done(((f32[2,128,128]{1,2,0:T(8,128)}), f32[2,128,128]{1,2,0:T(8,128)}) %all-reduce.3.cloned.1.call-update) | async-done | bytes 131088 | tf_op jit(solution)/shard_map/psum | solution.py:66
  373.3 0.9 broadcast_multiply_fusion.1
  374.4 0.9 fusion.49
  375.3 23.5 %custom-call.8 = f32[2,128,128]{2,1,0:T(8,128)S(1)} custom-call(f32[2,128,128]{2,1,0:T(8,128)S(1)} %fusion.49), custom_call_target="Cholesky" | custom-call | tf_op jit(solution)/shard_map/jit(cholesky)/cholesky | solution.py:54
  399.0 19.7 %custom-call.9 = f32[2,1,128,128]{2,3,1,0:T(8,128)S(1)} custom-call(f32[2,1,128,128]{3,2,1,0:T(8,128)S(1)} %select_bitcast_fusion.1), custom_call_target="InvertDiagBlocksLowerTriangular" | custom-call | tf_op jit(solution)/shard_map/triangular_solve/custom-call.0 | solution.py:59
  419.4 45.8 %all_gather.15 = f32[2,512,128]{2,1,0:T(8,128)S(1)} all-gather(f32[2,64,128]{2,1,0:T(8,128)S(1)} %fusion.63), channel_id=1, replica_groups=mesh['dof'=64,'real'=8] {'real'}, dimensions={1}, use_global_device_ids=true | all-gather | bytes 589824 | tf_op jit(solution)/shard_map/all_gather | solution.py:108
  465.7 1.1 fusion.64
  466.8 107.2 %all-reduce.5.cloned.1.call-done = f32[2,128,128]{1,2,0:T(8,128)} async-done(((f32[2,128,128]{1,2,0:T(8,128)}), f32[2,128,128]{1,2,0:T(8,128)}) %all-reduce.5.cloned.1.call-update) | async-done | bytes 131088 | tf_op jit(solution)/shard_map/psum | solution.py:66
  574.0 0.9 broadcast_multiply_fusion
  575.1 0.9 fusion.46
  576.0 23.5 %custom-call.10 = f32[2,128,128]{2,1,0:T(8,128)S(1)} custom-call(f32[2,128,128]{2,1,0:T(8,128)S(1)} %fusion.46), custom_call_target="Cholesky" | custom-call | tf_op jit(solution)/shard_map/jit(cholesky)/cholesky | solution.py:54
  599.7 19.7 %custom-call.11 = f32[2,1,128,128]{2,3,1,0:T(8,128)S(1)} custom-call(f32[2,1,128,128]{3,2,1,0:T(8,128)S(1)} %select_bitcast_fusion), custom_call_target="InvertDiagBlocksLowerTriangular" | custom-call | tf_op jit(solution)/shard_map/triangular_solve/custom-call.0 | solution.py:59
  619.8 1.0 fusion.65
  (59 shorter events, 9.8 us)
Async XLA Ops:
  7.2 249.2 %copy-start = (f32[2,4]{1,0:T(2,128)S(1)}, f32[2,4]{1,0:T(2,128)}, u32[]{:S(2)}) copy-start(f32[2,4]{1,0:T(2,128)} %param.17) | copy-start | bytes 100
  7.2 237.0 %all-gather.3.cloned.1.call-start = ((), (), s32[]{:S(2)}) async-start(), calls=%async_computation.2 | async-start | bytes 34078720 | tf_op jit(solution)/shard_map/all_gather | solution.py:88
  8.3 15.1 %collective-permute-start = (bf16[256,512]{1,0:T(8,128)(2,1)S(1)}, bf16[256,512]{1,0:T(8,128)(2,1)S(1)}, u32[]{:S(2)}, u32[]{:S(2)}) collective-permute-start(bf16[256,512]{1,0:T(8,128)(2,1)S(1)} %get-tuple-element.19), channel_id=1, source_target_pairs={{0,8},{8,16},{16,24},{24,32},{32,40},{40,48},{48,56},{56,64},{64,7... | collective-permute-start | bytes 786440 | tf_op jit(solution)/shard_map/ppermute | solution.py:17
  10.2 13.2 %collective-permute-start.1 = (bf16[256,512]{1,0:T(8,128)(2,1)S(1)}, bf16[256,512]{1,0:T(8,128)(2,1)}, u32[]{:S(2)}, u32[]{:S(2)}) collective-permute-start(bf16[256,512]{1,0:T(8,128)(2,1)S(1)} %get-tuple-element.20), channel_id=1, source_target_pairs={{8,0},{16,8},{24,16},{32,24},{40,32},{48,40},{56,48},{64,56},{72,6... | collective-permute-start | bytes 786440 | tf_op jit(solution)/shard_map/ppermute | solution.py:20
  18.0 5.4 copy-start.5
  34.6 2.7 copy-start.3
  34.6 3.2 copy-start.6
  37.8 1.6 copy-start.2
  39.4 1.6 copy-start.4
  41.0 1.6 copy-start.1
  42.5 1.6 copy-start.8
  42.5 1.6 copy-start.9
  42.5 1.6 copy-start.10
  44.1 2.9 copy-start.11
  46.2 327.1 %all-reduce.3.cloned.1.call-start = ((), (), s32[]{:S(2)}) async-start(), calls=%async_computation | async-start | bytes 262144 | tf_op jit(solution)/shard_map/psum | solution.py:66
  256.3 208.9 %copy-start.7 = (f32[256,512]{1,0:T(8,128)}, f32[256,512]{1,0:T(8,128)S(1)}, u32[]{:S(2)}) copy-start(f32[256,512]{1,0:T(8,128)S(1)} %reduce_sum.9) | copy-start | bytes 1572868
  259.2 314.8 %all-reduce.5.cloned.1.call-start = ((), (), s32[]{:S(2)}) async-start(), calls=%async_computation.1 | async-start | bytes 262144 | tf_op jit(solution)/shard_map/psum | solution.py:66
Sparse Core Ops, SparseCore 0:
  46.4 197.8 all-gather.2
  259.3 113.9 all-reduce.2
  466.9 107.0 all-reduce.4
